TPU v7x, 32 devices: a whole 2x2x4 slice. The times are simulated.
32 devices in a mesh: wave: 8 (over y, x, core), lev: 4 (over z).
Axes of the slice: x: 2, y: 2, z: 4, core: 2. Of those that a mesh axis runs over, the one named last changes fastest.
Arguments:
- spec: bfloat16 [16, 128, 640], P('wave', 'lev'), may hold values from -1.5 to 1.5
- legendre: bfloat16 [16, 1280, 640], P('wave'), may hold values from -0.25 to 0.25
- layer_depth_share: float32 [16], P('lev'), may hold values from 0.5 to 2
- quad_weight: float32 [1280], replicated, may hold values from 8 to 32
- wave_of_slot: int32 [16], P('wave'), may hold values from 0 to 639, as said below
Outputs:
- tendency: bfloat16 [16, 128, 640], P('wave', 'lev')
Inputs may be any that keep to these rules, and one draw needn't show every extreme that they name: `wave_of_slot`: slots 2 i and 2 i + 1 hold wavenumbers m and 639 - m; no wavenumber appears twice.
All inputs are finite; a program needn't handle non-finite values.
Results may differ from a plain program's by a relative error of at most 0.0047.
The roundings to bfloat16 on the way count: a program that leaves them out, or rounds other values in their place, can miss the bound.
Values may be sent and summed in bfloat16 or wider, within the bound.
A program may use at most 128 MiB of HBM per device.

v0:
```python
import functools
import math

import jax
import jax.numpy as jnp
import numpy as np
from jax import lax
from jax.experimental import pallas as pl
from jax.experimental.pallas import tpu as pltpu
from jax.sharding import PartitionSpec as P

TILES = 4
LANES = 128
NT = (((1,), (1,)), ((), ()))


def taylor(first, count):
    return [(-1.0) ** k / math.factorial(2 * k + first) for k in range(count)]


def horner(square, terms):
    total = jnp.full_like(square, terms[-1])
    for term in reversed(terms[:-1]):
        total = total * square + term
    return total


def turn_trig(steps, length, inverse):
    whole = jnp.floor(steps * inverse + 0.5)
    angle = (steps - whole * length) * inverse * (2.0 * math.pi)
    square = angle * angle
    return horner(square, taylor(0, 10)), angle * horner(square, taylor(1, 10))


def lane_maps(slots, fields, layers):
    order = np.arange(slots * 2 * 2 * fields * layers)
    natural = order.reshape(slots, 2, 2, fields, layers)
    return natural.transpose(0, 2, 3, 1, 4).reshape(-1)


def fourier_stage(dims, spec_ref, leg_ref, live_ref, perm_ref, rows_ref):
    slots, columns, half = dims["slots"], dims["columns"], dims["half"]
    total = jnp.zeros((half, LANES), jnp.float32)
    for slot in range(slots):
        masked = spec_ref[slot] * live_ref[slot]
        for hemi in range(2):
            at = (slot * 2 + hemi) * columns
            pieces = []
            if at:
                pieces.append(jnp.zeros((at, masked.shape[1]), masked.dtype))
            pieces.append(masked)
            if at + columns < LANES:
                pieces.append(jnp.zeros((LANES - at - columns, masked.shape[1]), masked.dtype))
            total += lax.dot_general(
                leg_ref[slot, hemi * half : (hemi + 1) * half, :],
                jnp.concatenate(pieces, 0),
                NT,
                preferred_element_type=jnp.float32,
            )
    rows_ref[...] = jnp.dot(
        total.astype(jnp.bfloat16), perm_ref[...], preferred_element_type=jnp.float32
    )


def split_rows(dims, rows_ref, send_ref):
    quarter, half = dims["quarter"], dims["half"]
    for place in range(dims["groups"]):
        low = rows_ref[place * quarter : (place + 1) * quarter, :]
        top = half - place * quarter
        high = rows_ref[top - quarter : top, :]
        send_ref[place] = jnp.concatenate([low, high], 0).astype(jnp.bfloat16)


def grid_stage(dims, device, waves, quad_ref, cor_ref, get_ref, put_refs, scratch):
    slots, groups, half = dims["slots"], dims["groups"], dims["half"]
    fields, layers, quarter = dims["fields"], dims["layers"], dims["quarter"]
    block, total_lat = dims["block"], 2 * half
    count = 2 * quarter
    width = fields * 2 * layers
    depth = 2 * slots * groups
    state, step, tab, left, mixed, acc = scratch
    chunk = TILES * LANES
    lane = lax.broadcasted_iota(jnp.int32, (groups, LANES), 1)
    south_lane = lane // layers % 2 == 1
    tile_lane = lax.broadcasted_iota(jnp.int32, (slots * groups, LANES), 1)
    tile_lane_f = tile_lane.astype(jnp.float32)
    hemi_row = lax.broadcasted_iota(jnp.int32, (2 * layers, 1), 0) < layers
    size = block * width
    padded = left.shape[0]
    eye = (
        lax.broadcasted_iota(jnp.int32, (padded, padded), 0)
        == lax.broadcasted_iota(jnp.int32, (padded, padded), 1)
    ).astype(jnp.bfloat16)
    mixed[...] = jnp.zeros_like(mixed)
    all_waves = jnp.concatenate(waves, 0)

    def group(number, carry):
        first = number * block
        local = [first + u for u in range(block)]
        dist = [
            jnp.where(r < quarter, device * quarter + r, half - device * quarter - count + r)
            for r in local
        ]
        lengths = [20 + 4 * q for q in dist]
        floats = [length.astype(jnp.float32) for length in lengths]
        for u in range(block):
            inverse = 1.0 / jnp.full((slots * groups, LANES), floats[u], jnp.float32)
            rows = pl.ds(u * slots * groups, slots * groups)
            base = turn_trig(all_waves * tile_lane_f, floats[u], inverse)
            hop = turn_trig(all_waves * float(LANES), floats[u], inverse)
            for part in range(2):
                state[part, rows, :] = base[part]
                step[part, rows, :] = hop[part]
            north = get_ref[pl.ds(local[u], groups, stride=count), :]
            south = get_ref[pl.ds(count - 1 - local[u], groups, stride=count), :]
            both = jnp.where(south_lane, south, north)
            at = u * width
            column = at // LANES * LANES
            offset = at % LANES
            for part in range(2):
                for slot in range(slots):
                    home = (slot * 2 + part) * width
                    wave = waves[slot]
                    weight = jnp.where(wave == 0.0, 1.0, 2.0)
                    weight = jnp.where(2.0 * wave < floats[u], weight, 0.0)
                    if part:
                        weight = -weight
                    shift = (offset - home) % LANES
                    moved = pltpu.roll(both, shift, 1) if shift else both
                    keep = (lane >= offset) & (lane < offset + width)
                    row = u * depth + (part * slots + slot) * groups
                    mixed[row : row + groups, column : column + LANES] = jnp.where(
                        keep, moved * weight, 0.0
                    )
        left[...] = lax.dot_general(
            eye, mixed[...].astype(jnp.bfloat16), NT, preferred_element_type=jnp.float32
        ).astype(jnp.bfloat16)
        acc[...] = jnp.zeros_like(acc)
        cor = [
            jnp.where(hemi_row, cor_ref[dist[u]], cor_ref[total_lat - 1 - dist[u]])
            for u in range(block)
        ]

        def walk(index, carry):
            cosine, sine = state[0], state[1]
            turn_cos, turn_sin = step[0], step[1]
            for t in range(TILES):
                start = index * chunk + t * LANES
                point = tile_lane + start
                for u in range(block):
                    rows = slice(u * slots * groups, (u + 1) * slots * groups)
                    live = point < lengths[u]
                    cols = slice(t * LANES, (t + 1) * LANES)
                    low = u * depth
                    mid = low + slots * groups
                    tab[low:mid, cols] = jnp.where(live, cosine[rows], 0.0).astype(jnp.bfloat16)
                    tab[mid : low + depth, cols] = jnp.where(live, sine[rows], 0.0).astype(
                        jnp.bfloat16
                    )
                cosine, sine = (
                    cosine * turn_cos - sine * turn_sin,
                    sine * turn_cos + cosine * turn_sin,
                )
            state[0], state[1] = cosine, sine
            table = tab[...]
            grid = jnp.dot(left[...], table, preferred_element_type=jnp.float32)
            made = []
            for u in range(block):
                part = [
                    grid[u * width + f * 2 * layers : u * width + (f + 1) * 2 * layers]
                    for f in range(fields)
                ]
                absolute = part[2] + cor[u]
                made += [
                    absolute * part[0],
                    absolute * part[1],
                    0.5 * (part[0] * part[0] + part[1] * part[1]),
                    part[0] * part[3],
                ]
            if padded > size:
                made.append(jnp.zeros((padded - size, chunk), jnp.float32))
            products = jnp.concatenate(made, 0).astype(jnp.bfloat16)
            acc[...] += lax.dot_general(table, products, NT, preferred_element_type=jnp.float32)
            return carry

        longest = lengths[-1]
        lax.fori_loop(0, (longest + chunk - 1) // chunk, walk, 0)
        for u in range(block):
            at = u * width
            column = at // LANES * LANES
            offset = at % LANES
            north = quad_ref[dist[u]]
            south = quad_ref[total_lat - 1 - dist[u]]
            scale = jnp.where(south_lane, south, north) / floats[u]
            joined = jnp.zeros((groups, LANES), jnp.float32)
            for part in range(2):
                for slot in range(slots):
                    home = (slot * 2 + part) * width
                    row = u * depth + (part * slots + slot) * groups
                    value = acc[row : row + groups, column : column + LANES]
                    shift = (home - offset) % LANES
                    value = pltpu.roll(value, shift, 1) if shift else value
                    keep = (lane >= home) & (lane < home + width)
                    keep = keep & (2.0 * waves[slot] < floats[u])
                    joined = joined + jnp.where(keep, -value if part else value, 0.0)
            joined = joined * scale
            put_refs[0][pl.ds(local[u], groups, stride=count), :] = joined
            put_refs[1][pl.ds(count - 1 - local[u], groups, stride=count), :] = joined
        return carry

    lax.fori_loop(0, count // block, group, 0)


def grid_scratch(dims):
    slots, groups, block = dims["slots"], dims["groups"], dims["block"]
    rows = block * slots * groups
    padded = -(-block * dims["fields"] * 2 * dims["layers"] // LANES) * LANES
    return [
        pltpu.VMEM((2, rows, LANES), jnp.float32),
        pltpu.VMEM((2, rows, LANES), jnp.float32),
        pltpu.VMEM((2 * rows, TILES * LANES), jnp.bfloat16),
        pltpu.VMEM((padded, 2 * rows), jnp.bfloat16),
        pltpu.VMEM((2 * rows, padded), jnp.float32),
        pltpu.VMEM((2 * rows, padded), jnp.float32),
    ]


def final_stage(dims, get, leg_ref, perm_ref):
    slots, columns, half = dims["slots"], dims["columns"], dims["half"]
    turned = lax.dot_general(
        perm_ref[...], get, NT, preferred_element_type=jnp.float32
    ).astype(jnp.bfloat16)
    results = []
    for slot in range(slots):
        total = 0.0
        for hemi in range(2):
            at = (slot * 2 + hemi) * columns
            total += jnp.dot(
                turned[at : at + columns],
                leg_ref[slot, hemi * half : (hemi + 1) * half, :],
                preferred_element_type=jnp.float32,
            )
        results.append(total)
    return results


def joined_rows(dims, back_ref):
    quarter, groups = dims["quarter"], dims["groups"]
    low = [back_ref[place][:quarter] for place in range(groups)]
    high = [back_ref[place][quarter:] for place in reversed(range(groups))]
    return low + high


def first_kernel(dims, spec_ref, leg_ref, live_ref, perm_ref, out_ref, rows_ref):
    fourier_stage(dims, spec_ref, leg_ref, live_ref, perm_ref, rows_ref)
    split_rows(dims, rows_ref, out_ref)


def middle_kernel(dims, recv_ref, waves_ref, quad_ref, cor_ref, out_ref, get, north, south, *scratch):
    groups, count = dims["groups"], 2 * dims["quarter"]
    for source in range(groups):
        get[source * count : (source + 1) * count, :] = recv_ref[source].astype(jnp.float32)
    waves = [waves_ref[slot] for slot in range(dims["slots"])]
    device = lax.axis_index("wave")
    grid_stage(dims, device, waves, quad_ref, cor_ref, get, (north, south), scratch)
    hemi = lax.broadcasted_iota(jnp.int32, (count, LANES), 1) // dims["layers"] % 2
    for source in range(groups):
        rows = slice(source * count, (source + 1) * count)
        out_ref[source] = jnp.where(hemi == 1, south[rows], north[rows]).astype(jnp.bfloat16)


def last_kernel(dims, back_ref, leg_ref, live_ref, perm_ref, geo_ref, out_ref):
    rows = [piece.astype(jnp.float32) for piece in joined_rows(dims, back_ref)]
    get = jnp.concatenate(rows, 0).astype(jnp.bfloat16)
    for slot, value in enumerate(final_stage(dims, get, leg_ref, perm_ref)):
        live = live_ref[slot].astype(jnp.float32)
        out_ref[slot] = ((value + geo_ref[slot]) * live).astype(jnp.bfloat16)


def body(spec, legendre, layer_depth_share, quad_weight, wave_of_slot):
    slots, columns, degrees = spec.shape
    total_lat = legendre.shape[1]
    groups = lax.axis_size("wave")
    layers = layer_depth_share.shape[0]
    quarter = total_lat // groups // 4
    depth = 2 * slots * groups
    block = max(b for b in range(1, quarter + 1) if quarter % b == 0 and b * depth <= max(256, depth))
    dims = dict(
        slots=slots, columns=columns, half=total_lat // 2, groups=groups, layers=layers,
        fields=columns // (2 * layers), quarter=quarter, block=block,
    )
    fields = dims["fields"]
    maps = lane_maps(slots, fields, layers)
    perm = np.zeros((LANES, LANES), np.float32)
    perm[maps, np.arange(LANES)] = 1.0
    perm = jnp.asarray(perm, jnp.bfloat16)
    lat = np.arange(total_lat)
    coriolis = jnp.asarray(2.0 * np.cos(np.pi * (lat + 0.5) / total_lat), jnp.float32)
    all_waves = lax.all_gather(wave_of_slot, "wave")
    waves = jnp.broadcast_to(
        all_waves.T.astype(jnp.float32)[:, :, None], (slots, groups, LANES)
    )
    degree = jnp.arange(degrees, dtype=jnp.int32)
    alive = degree[None, None, :] < (degrees - wave_of_slot)[:, None, None]
    live = alive.astype(jnp.bfloat16)
    thermal = jnp.where(alive, spec, 0).reshape(slots, 2, fields, layers, degrees)[:, :, 3]
    scaled = thermal.astype(jnp.float32) * layer_depth_share[None, None, :, None]
    below = jnp.flip(jnp.cumsum(jnp.flip(scaled, 2), 2), 2)
    parts = lax.all_gather(below[:, :, 0], "lev")
    place = jnp.arange(parts.shape[0]) > lax.axis_index("lev")
    deeper = jnp.sum(jnp.where(place[:, None, None, None], parts, 0.0), 0)
    geopot = below + deeper[:, :, None]
    geo = jnp.zeros((slots, 2, fields, layers, degrees), jnp.float32)
    geo = geo.at[:, :, 2].set(geopot).reshape(slots, columns, degrees)
    vmem = pl.BlockSpec(memory_space=pltpu.VMEM)
    smem = pl.BlockSpec(memory_space=pltpu.SMEM)
    count = 2 * quarter
    send = pl.pallas_call(
        functools.partial(first_kernel, dims),
        out_shape=jax.ShapeDtypeStruct((groups, count, LANES), jnp.bfloat16),
        in_specs=[vmem] * 4,
        out_specs=vmem,
        scratch_shapes=[pltpu.VMEM((dims["half"], LANES), jnp.float32)],
    )(spec, legendre, live, perm)
    recv = lax.all_to_all(send, "wave", 0, 0)
    flat = pltpu.VMEM((groups * count, LANES), jnp.float32)
    out = pl.pallas_call(
        functools.partial(middle_kernel, dims),
        out_shape=jax.ShapeDtypeStruct((groups, count, LANES), jnp.bfloat16),
        in_specs=[vmem, vmem, smem, smem],
        out_specs=vmem,
        scratch_shapes=[flat, flat, flat] + grid_scratch(dims),
    )(recv, waves, quad_weight, coriolis)
    back = lax.all_to_all(out, "wave", 0, 0)
    return pl.pallas_call(
        functools.partial(last_kernel, dims),
        out_shape=jax.ShapeDtypeStruct(spec.shape, jnp.bfloat16),
        in_specs=[vmem] * 5,
        out_specs=vmem,
    )(back, legendre, live, perm, geo)


def solution(mesh):
    in_specs = (P("wave", "lev", None), P("wave", None, None), P("lev"), P(), P("wave"))
    out_specs = P("wave", "lev", None)
    return jax.shard_map(body, mesh=mesh, in_specs=in_specs, out_specs=out_specs, check_vma=False)
```

profile of v0, /device:TPU:0, one launch (start us, length us, event | category | flops | bytes accessed | tf_op | source)
XLA Modules:
  0.0 71.5 jit_solution(11400596858000833393)
XLA Ops:
  0.0 0.0 copy-start.5
  0.0 0.0 copy-start.4
  0.0 0.0 copy-start.2
  0.0 0.0 copy-start.3
  0.0 0.7 %broadcast_subtract_fusion = s32[2]{0:T(128)S(1)} fusion(s32[2]{0:T(128)} %param.13), kind=kLoop, calls=%fused_computation.8 | loop fusion | flops 2 | bytes 16 | tf_op jit(solution)/shard_map/sub | solution.py:304
  0.7 0.7 compare_convert_fusion.live_ref
  1.4 3.7 %shard_map.73 = bf16[8,80,128]{2,1,0:T(8,128)(2,1)} custom-call(bf16[2,32,640]{2,1,0:T(8,128)(2,1)} %spec_ref.1, bf16[2,1280,640]{2,1,0:T(8,128)(2,1)} %leg_ref.3, bf16[2,1,640]{2,1,0:T(2,128)(2,1)} %compare_convert_fusion.live_ref, bf16[128,128]{1,0:T(8,128)(2,1)} %constant.45.clone.perm_ref), custom_call_target="tpu_custom_call" | custom-call | tf_op jit(solution)/shard_map/pallas_call | solution.py:318
  5.1 5.2 %all-to-all-start = ((bf16[8,80,128]{2,1,0:T(8,128)(2,1)}), bf16[8,80,128]{2,1,0:T(8,128)(2,1)S(1)}, u32[]{:S(2)}, u32[]{:S(2)}) async-start(bf16[8,80,128]{2,1,0:T(8,128)(2,1)} %shard_map.73), calls=%async_computation | async-start | bytes 327680 | tf_op jit(solution)/shard_map/all_to_all | solution.py:325
  10.3 0.1 iota_compare_fusion
  10.4 0.0 copy-done.2
  10.4 0.1 copy.19
  10.5 0.0 copy-done.3
  10.5 0.1 convert_multiply_fusion
  10.7 0.0 copy-done.5
  10.7 0.6 dynamic-slice.7
  11.9 0.0 copy-done.4
  11.9 0.2 dynamic-update-slice.3
  12.2 8.5 %all-reduce.1 = s32[16]{0:T(128)S(1)} all-reduce(s32[16]{0:T(128)S(1)} %dynamic-update-slice.3), channel_id=2, replica_groups=mesh['wave'=8,'lev'=4] {'wave'}, use_global_device_ids=true, to_apply=%add.1 | all-reduce | flops 16 | bytes 128
  20.7 0.1 reshape.112
  20.8 0.1 copy.18
  20.9 13.4 %all-gather.1 = f32[8,2,1,640]{3,1,2,0:T(2,128)S(1)} all-gather(f32[2,2,1,640]{3,1,2,0:T(2,128)S(1)} %copy.20), channel_id=3, replica_groups=mesh['wave'=8,'lev'=4] {'lev'}, dimensions={0}, use_global_device_ids=true | all-gather | bytes 51200 | tf_op jit(solution)/shard_map/all_gather | solution.py:309
  34.2 0.1 select_reduce_fusion
  34.3 0.0 all-to-all-done.recv_ref
  34.3 0.0 copy-start.1
  34.4 0.7 broadcast_in_dim.36.waves_ref
  35.0 0.0 copy-done.1
  35.0 23.3 %shard_map.74 = bf16[8,80,128]{2,1,0:T(8,128)(2,1)} custom-call(bf16[8,80,128]{2,1,0:T(8,128)(2,1)} %copy-done.1, f32[2,8,128]{2,1,0:T(8,128)} %broadcast_in_dim.36.waves_ref, f32[1280]{0:T(1024)} %quad_ref.1, f32[1280]{0:T(1024)} %constant.46.clone.cor_ref), custom_call_target="tpu_custom_call" | custom-call | tf_op jit(solution)/shard_map/pallas_call | solution.py:327
  58.3 3.4 %all-to-all-start.1 = ((bf16[8,80,128]{2,1,0:T(8,128)(2,1)}), bf16[8,80,128]{2,1,0:T(8,128)(2,1)S(1)}, u32[]{:S(2)}, u32[]{:S(2)}) async-start(bf16[8,80,128]{2,1,0:T(8,128)(2,1)} %shard_map.74), calls=%async_computation.1 | async-start | bytes 327680 | tf_op jit(solution)/shard_map/all_to_all | solution.py:334
  61.8 0.7 reshape.108.geo_ref
  62.5 5.0 %all-to-all-done.1.back_ref = bf16[8,80,128]{2,1,0:T(8,128)(2,1)S(1)} async-done(((bf16[8,80,128]{2,1,0:T(8,128)(2,1)}), bf16[8,80,128]{2,1,0:T(8,128)(2,1)S(1)}, u32[]{:S(2)}, u32[]{:S(2)}) %all-to-all-start.1) | async-done | bytes 163872 | tf_op jit(solution)/shard_map/all_to_all | solution.py:334
  67.5 0.7 copy-done
  68.1 3.4 %shard_map.75 = bf16[2,32,640]{2,1,0:T(8,128)(2,1)} custom-call(bf16[8,80,128]{2,1,0:T(8,128)(2,1)} %copy-done, bf16[2,1280,640]{2,1,0:T(8,128)(2,1)} %leg_ref.3, bf16[2,1,640]{2,1,0:T(2,128)(2,1)} %compare_convert_fusion.live_ref, bf16[128,128]{1,0:T(8,128)(2,1)} %constant.45.clone.perm_ref, f32[2,32,640]{2,1,0:T(8,128)} %reshape.108.geo_ref), custom_call_target="tpu_custom_call" | custom-call | tf_op jit(solution)/shard_map/pallas_call | solution.py:335
  (13 shorter events, 0.1 us)
Async XLA Ops:
  0.0 10.7 %copy-start.5 = (u32[32]{0:T(128)S(1)}, u32[32]{0:T(128)}, u32[]{:S(2)}) copy-start(u32[32]{0:T(128)} %constant.54) | copy-start | bytes 388
  0.0 11.9 %copy-start.4 = (s32[2]{0:T(128)S(1)}, s32[2]{0:T(128)}, u32[]{:S(2)}) copy-start(s32[2]{0:T(128)} %param.13) | copy-start | bytes 28
  0.0 10.4 %copy-start.2 = (bf16[2,32,640]{2,1,0:T(8,128)(2,1)S(1)}, bf16[2,32,640]{2,1,0:T(8,128)(2,1)}, u32[]{:S(2)}) copy-start(bf16[2,32,640]{2,1,0:T(8,128)(2,1)} %spec_ref.1) | copy-start | bytes 245764
  0.0 10.5 %copy-start.3 = (f32[4]{0:T(128)S(1)}, f32[4]{0:T(128)}, u32[]{:S(2)}) copy-start(f32[4]{0:T(128)} %param.11) | copy-start | bytes 52
  5.1 29.2 %all-to-all-start = ((bf16[8,80,128]{2,1,0:T(8,128)(2,1)}), bf16[8,80,128]{2,1,0:T(8,128)(2,1)S(1)}, u32[]{:S(2)}, u32[]{:S(2)}) async-start(bf16[8,80,128]{2,1,0:T(8,128)(2,1)} %shard_map.73), calls=%async_computation | async-start | bytes 327680 | tf_op jit(solution)/shard_map/all_to_all | solution.py:325
  34.3 0.7 copy-start.1
  58.3 9.2 %all-to-all-start.1 = ((bf16[8,80,128]{2,1,0:T(8,128)(2,1)}), bf16[8,80,128]{2,1,0:T(8,128)(2,1)S(1)}, u32[]{:S(2)}, u32[]{:S(2)}) async-start(bf16[8,80,128]{2,1,0:T(8,128)(2,1)} %shard_map.74), calls=%async_computation.1 | async-start | bytes 327680 | tf_op jit(solution)/shard_map/all_to_all | solution.py:334
  67.5 0.7 copy-start
where the time goes:
time: 71.9 us; the launch traced here: 71.5 us
  Pallas kernels  30.4 us (42%)
  blocking collectives  21.9 us (30%)
  starting transfers between devices  8.58 us (12%)
  waiting for transfers between devices  5 us (7%)
  local copies, waits for them, and re-layouts  3.17 us (4%)
  other arithmetic  1.7 us (2%)
  between operations  0.8 us (1%)
    pallas_call x1, Pallas kernels, body(): pl.pallas_call(functools.partial(middle_kernel, dims), out_shape=jax.Shap...  23.3 us
    all_gather x1, blocking collectives, body(): parts = lax.all_gather(below[:, :, 0], 'lev')  13.4 us
    unnamed x1, blocking collectives  8.49 us
    all_to_all x1, starting transfers between devices, body(): recv = lax.all_to_all(send, 'wave', 0, 0)  5.2 us
    all_to_all x1, waiting for transfers between devices, body(): back = lax.all_to_all(out, 'wave', 0, 0)  5 us
    pallas_call x1, Pallas kernels, body(): pl.pallas_call(functools.partial(first_kernel, dims), out_shape=jax.Shape...  3.74 us
    all_to_all x1, starting transfers between devices, body(): back = lax.all_to_all(out, 'wave', 0, 0)  3.38 us
    pallas_call x1, Pallas kernels, body(): pl.pallas_call(functools.partial(last_kernel, dims), out_shape=jax.ShapeD...  3.37 us
  transfers between devices with their start and end apart: 2, of which 1 were waited for; matrix products, arithmetic and copies ran while one was open for 3% of the time, Pallas kernels for 0%

commit v1 on v0

--- a/solution.py
+++ b/solution.py
@@ -38,11 +38,11 @@
     return natural.transpose(0, 2, 3, 1, 4).reshape(-1)
 
 
-def fourier_stage(dims, spec_ref, leg_ref, live_ref, perm_ref, rows_ref):
+def fourier_stage(dims, spec_ref, leg_ref, loads, live, perm_ref, rows_ref):
     slots, columns, half = dims["slots"], dims["columns"], dims["half"]
     total = jnp.zeros((half, LANES), jnp.float32)
     for slot in range(slots):
-        masked = spec_ref[slot] * live_ref[slot]
+        masked = spec_ref[slot] * live[slot].astype(jnp.bfloat16)
         for hemi in range(2):
             at = (slot * 2 + hemi) * columns
             pieces = []
@@ -51,6 +51,7 @@
             pieces.append(masked)
             if at + columns < LANES:
                 pieces.append(jnp.zeros((LANES - at - columns, masked.shape[1]), masked.dtype))
+            loads[slot * 2 + hemi].wait()
             total += lax.dot_general(
                 leg_ref[slot, hemi * half : (hemi + 1) * half, :],
                 jnp.concatenate(pieces, 0),
@@ -251,30 +252,129 @@
     return low + high
 
 
-def first_kernel(dims, spec_ref, leg_ref, live_ref, perm_ref, out_ref, rows_ref):
-    fourier_stage(dims, spec_ref, leg_ref, live_ref, perm_ref, rows_ref)
-    split_rows(dims, rows_ref, out_ref)
-
-
-def middle_kernel(dims, recv_ref, waves_ref, quad_ref, cor_ref, out_ref, get, north, south, *scratch):
-    groups, count = dims["groups"], 2 * dims["quarter"]
+def to_peer(axis, shift):
+    place = lax.axis_index(axis)
+    count = lax.axis_size(axis)
+    return {axis: lax.rem(place + shift, count)}
+
+
+def exchange(axis, source_of, target_of, sems):
+    place = lax.axis_index(axis)
+    count = lax.axis_size(axis)
+    copies = []
+    for shift in range(1, count):
+        peer = lax.rem(place + shift, count)
+        copies.append(
+            pltpu.make_async_remote_copy(
+                src_ref=source_of(peer),
+                dst_ref=target_of(place),
+                send_sem=sems[0].at[shift],
+                recv_sem=sems[1].at[shift],
+                device_id=to_peer(axis, shift),
+                device_id_type=pl.DeviceIdType.MESH,
+            )
+        )
+    return copies
+
+
+def whole_kernel(
+    dims, spec_ref, leg_hbm, perm_ref, share_ref, quad_ref, cor_ref, wave_ref, out_ref,
+    leg, rows, send, recv, back_send, back, wave_send, wave_recv, sum_send, sum_recv, geo,
+    get, north, south, load_sem, sem_a, sem_b, sem_c, sem_d, sem_e, sem_f, sem_g, sem_h, *scratch,
+):
+    slots, groups, half = dims["slots"], dims["groups"], dims["half"]
+    fields, layers, count = dims["fields"], dims["layers"], 2 * dims["quarter"]
+    degrees = spec_ref.shape[2]
+    me = lax.axis_index("wave")
+    floor = lax.axis_index("lev")
+    floors = lax.axis_size("lev")
+    loads = []
+    for slot in range(slots):
+        for hemi in range(2):
+            piece = pl.ds(hemi * half, half)
+            copy = pltpu.make_async_copy(
+                leg_hbm.at[slot, piece], leg.at[slot, piece], load_sem.at[slot * 2 + hemi]
+            )
+            copy.start()
+            loads.append(copy)
+    barrier = pltpu.get_barrier_semaphore()
+    for axis, size in (("wave", groups), ("lev", floors)):
+        for shift in range(1, size):
+            pl.semaphore_signal(
+                barrier, inc=1, device_id=to_peer(axis, shift), device_id_type=pl.DeviceIdType.MESH
+            )
+    degree = lax.broadcasted_iota(jnp.int32, (1, degrees), 1)
+    live = [
+        jnp.where(degree < degrees - wave_ref[slot], 1.0, 0.0).astype(jnp.float32)
+        for slot in range(slots)
+    ]
+    row = lax.broadcasted_iota(jnp.int32, (8, LANES), 0)
+    own = jnp.zeros((8, LANES), jnp.float32)
+    for slot in range(slots):
+        own = jnp.where(row == slot, wave_ref[slot].astype(jnp.float32), own)
+    wave_send[...] = own
+    geo[...] = jnp.zeros_like(geo)
+    for slot in range(slots):
+        full = spec_ref[slot].astype(jnp.float32) * live[slot]
+        for part in range(2):
+            first = part * fields * layers
+            total = jnp.zeros((1, degrees), jnp.float32)
+            for layer in reversed(range(layers)):
+                at = first + 3 * layers + layer
+                total = total + full[at : at + 1] * share_ref[layer]
+                at = first + 2 * layers + layer
+                geo[slot, at : at + 1, :] = total
+            at = slot * 2 + part
+            sum_send[at : at + 1, :] = total
+    pl.semaphore_wait(barrier, groups - 1 + floors - 1)
+
+    def wave_place(device):
+        return wave_recv.at[pl.ds(pl.multiple_of(device * 8, 8), 8)]
+
+    tell = exchange("wave", lambda _: wave_send, wave_place, (sem_a, sem_b))
+    lift = exchange("lev", lambda _: sum_send, lambda p: sum_recv.at[p], (sem_c, sem_d))
+    for copy in tell + lift:
+        copy.start()
+    wave_recv[pl.ds(pl.multiple_of(me * 8, 8), 8), :] = own
+    fourier_stage(dims, spec_ref, leg, loads, live, perm_ref, rows)
+    split_rows(dims, rows, send)
+    there = exchange("wave", lambda p: send.at[p], lambda p: recv.at[p], (sem_e, sem_f))
+    for copy in there:
+        copy.start()
+    recv[me] = send[me]
+    for copy in tell:
+        copy.wait()
+    waves = [wave_recv[pl.ds(slot, groups, stride=8), :] for slot in range(slots)]
+    for copy in there:
+        copy.wait()
     for source in range(groups):
-        get[source * count : (source + 1) * count, :] = recv_ref[source].astype(jnp.float32)
-    waves = [waves_ref[slot] for slot in range(dims["slots"])]
-    device = lax.axis_index("wave")
-    grid_stage(dims, device, waves, quad_ref, cor_ref, get, (north, south), scratch)
-    hemi = lax.broadcasted_iota(jnp.int32, (count, LANES), 1) // dims["layers"] % 2
+        get[source * count : (source + 1) * count, :] = recv[source].astype(jnp.float32)
+    grid_stage(dims, me, waves, quad_ref, cor_ref, get, (north, south), scratch)
+    hemi = lax.broadcasted_iota(jnp.int32, (count, LANES), 1) // layers % 2
     for source in range(groups):
-        rows = slice(source * count, (source + 1) * count)
-        out_ref[source] = jnp.where(hemi == 1, south[rows], north[rows]).astype(jnp.bfloat16)
-
-
-def last_kernel(dims, back_ref, leg_ref, live_ref, perm_ref, geo_ref, out_ref):
-    rows = [piece.astype(jnp.float32) for piece in joined_rows(dims, back_ref)]
-    get = jnp.concatenate(rows, 0).astype(jnp.bfloat16)
-    for slot, value in enumerate(final_stage(dims, get, leg_ref, perm_ref)):
-        live = live_ref[slot].astype(jnp.float32)
-        out_ref[slot] = ((value + geo_ref[slot]) * live).astype(jnp.bfloat16)
+        piece = slice(source * count, (source + 1) * count)
+        back_send[source] = jnp.where(hemi == 1, south[piece], north[piece]).astype(jnp.bfloat16)
+    home = exchange("wave", lambda p: back_send.at[p], lambda p: back.at[p], (sem_g, sem_h))
+    for copy in home:
+        copy.start()
+    back[me] = back_send[me]
+    for copy in lift:
+        copy.wait()
+    for slot in range(slots):
+        for part in range(2):
+            at = slot * 2 + part
+            deeper = jnp.zeros((1, degrees), jnp.float32)
+            for other in range(floors):
+                value = sum_recv[other, at : at + 1, :]
+                deeper = deeper + jnp.where(other > floor, value, 0.0)
+            first = (part * fields + 2) * layers
+            geo[slot, first : first + layers, :] += deeper
+    for copy in home:
+        copy.wait()
+    pieces = [piece.astype(jnp.float32) for piece in joined_rows(dims, back)]
+    joined = jnp.concatenate(pieces, 0).astype(jnp.bfloat16)
+    for slot, value in enumerate(final_stage(dims, joined, leg, perm_ref)):
+        out_ref[slot] = ((value + geo[slot]) * live[slot]).astype(jnp.bfloat16)
 
 
 def body(spec, legendre, layer_depth_share, quad_weight, wave_of_slot):
@@ -296,48 +396,41 @@
     perm = jnp.asarray(perm, jnp.bfloat16)
     lat = np.arange(total_lat)
     coriolis = jnp.asarray(2.0 * np.cos(np.pi * (lat + 0.5) / total_lat), jnp.float32)
-    all_waves = lax.all_gather(wave_of_slot, "wave")
-    waves = jnp.broadcast_to(
-        all_waves.T.astype(jnp.float32)[:, :, None], (slots, groups, LANES)
-    )
-    degree = jnp.arange(degrees, dtype=jnp.int32)
-    alive = degree[None, None, :] < (degrees - wave_of_slot)[:, None, None]
-    live = alive.astype(jnp.bfloat16)
-    thermal = jnp.where(alive, spec, 0).reshape(slots, 2, fields, layers, degrees)[:, :, 3]
-    scaled = thermal.astype(jnp.float32) * layer_depth_share[None, None, :, None]
-    below = jnp.flip(jnp.cumsum(jnp.flip(scaled, 2), 2), 2)
-    parts = lax.all_gather(below[:, :, 0], "lev")
-    place = jnp.arange(parts.shape[0]) > lax.axis_index("lev")
-    deeper = jnp.sum(jnp.where(place[:, None, None, None], parts, 0.0), 0)
-    geopot = below + deeper[:, :, None]
-    geo = jnp.zeros((slots, 2, fields, layers, degrees), jnp.float32)
-    geo = geo.at[:, :, 2].set(geopot).reshape(slots, columns, degrees)
+    floors = lax.axis_size("lev")
+    half, count = total_lat // 2, 2 * quarter
     vmem = pl.BlockSpec(memory_space=pltpu.VMEM)
     smem = pl.BlockSpec(memory_space=pltpu.SMEM)
-    count = 2 * quarter
-    send = pl.pallas_call(
-        functools.partial(first_kernel, dims),
-        out_shape=jax.ShapeDtypeStruct((groups, count, LANES), jnp.bfloat16),
-        in_specs=[vmem] * 4,
+    rows = pltpu.VMEM((groups, count, LANES), jnp.bfloat16)
+    flat = pltpu.VMEM((groups * count, LANES), jnp.float32)
+    sums = 2 * slots
+    return pl.pallas_call(
+        functools.partial(whole_kernel, dims),
+        out_shape=jax.ShapeDtypeStruct(spec.shape, jnp.bfloat16),
+        in_specs=[vmem, pl.BlockSpec(memory_space=pl.ANY), vmem] + [smem] * 4,
         out_specs=vmem,
-        scratch_shapes=[pltpu.VMEM((dims["half"], LANES), jnp.float32)],
-    )(spec, legendre, live, perm)
-    recv = lax.all_to_all(send, "wave", 0, 0)
-    flat = pltpu.VMEM((groups * count, LANES), jnp.float32)
-    out = pl.pallas_call(
-        functools.partial(middle_kernel, dims),
-        out_shape=jax.ShapeDtypeStruct((groups, count, LANES), jnp.bfloat16),
-        in_specs=[vmem, vmem, smem, smem],
-        out_specs=vmem,
-        scratch_shapes=[flat, flat, flat] + grid_scratch(dims),
-    )(recv, waves, quad_weight, coriolis)
-    back = lax.all_to_all(out, "wave", 0, 0)
-    return pl.pallas_call(
-        functools.partial(last_kernel, dims),
-        out_shape=jax.ShapeDtypeStruct(spec.shape, jnp.bfloat16),
-        in_specs=[vmem] * 5,
-        out_specs=vmem,
-    )(back, legendre, live, perm, geo)
+        scratch_shapes=[
+            pltpu.VMEM(legendre.shape, jnp.bfloat16),
+            pltpu.VMEM((half, LANES), jnp.float32),
+            rows, rows, rows, rows,
+            pltpu.VMEM((8, LANES), jnp.float32),
+            pltpu.VMEM((groups * 8, LANES), jnp.float32),
+            pltpu.VMEM((sums, degrees), jnp.float32),
+            pltpu.VMEM((floors, sums, degrees), jnp.float32),
+            pltpu.VMEM(spec.shape, jnp.float32),
+            flat, flat, flat,
+            pltpu.SemaphoreType.DMA((2 * slots,)),
+            pltpu.SemaphoreType.DMA((groups,)),
+            pltpu.SemaphoreType.DMA((groups,)),
+            pltpu.SemaphoreType.DMA((floors,)),
+            pltpu.SemaphoreType.DMA((floors,)),
+            pltpu.SemaphoreType.DMA((groups,)),
+            pltpu.SemaphoreType.DMA((groups,)),
+            pltpu.SemaphoreType.DMA((groups,)),
+            pltpu.SemaphoreType.DMA((groups,)),
+        ]
+        + grid_scratch(dims),
+        compiler_params=pltpu.CompilerParams(collective_id=0, has_side_effects=True),
+    )(spec, legendre, perm, layer_depth_share, quad_weight, coriolis, wave_of_slot)
 
 
 def solution(mesh):

time: 71.9 us -> 40.9 us (0.57)
  blocking collectives: 21.9 us -> 0 us
  Pallas kernels: 30.4 us -> 39.2 us
  starting transfers between devices: 8.58 us -> 0 us
  waiting for transfers between devices: 5 us -> 0 us
  other arithmetic: 1.7 us -> 0 us
  local copies, waits for them, and re-layouts: 3.17 us -> 1.53 us
  between operations: 0.8 us -> 0.01 us
    all_gather x1 -> x0, blocking collectives: 13.4 us -> none  [body(): parts = lax.all_gather(below[:, :, 0], 'lev')]
    pallas_call x3 -> x1, Pallas kernels: 30.4 us -> 39.2 us  [body(): pl.pallas_call(functools.partial(whole_kernel, dims), out_shape=jax.Shape...]
    all_to_all x2 -> x0, starting transfers between devices: 8.58 us -> none  [the longest x1 5.2 us: body(): recv = lax.all_to_all(send, 'wave', 0, 0)]
    unnamed x1 -> x0, blocking collectives: 8.49 us -> none
    all_to_all x2 -> x0, waiting for transfers between devices: 5 us -> none  [the longest x1 5 us: body(): back = lax.all_to_all(out, 'wave', 0, 0)]
    sub x1 -> x0, other arithmetic: 0.72 us -> none  [body(): alive = degree[None, None, :] < (degrees - wave_of_slot)[:, None, None]]
    unnamed x16 -> x1, local copies, waits for them, and re-layouts: 1.52 us -> 1.53 us
  transfers between devices with their start and end apart: 2 -> 0, of which waited for: 1 -> 0; matrix products, arithmetic and copies ran while one was open for 3% -> 0% of each run, Pallas kernels for 0% -> 0%
where the time goes in v1:
time: 40.9 us; the launch traced here: 40.8 us
  Pallas kernels  39.2 us (96%)
  local copies, waits for them, and re-layouts  1.53 us (4%)
    pallas_call x1, Pallas kernels, body(): pl.pallas_call(functools.partial(whole_kernel, dims), out_shape=jax.Shape...  39.2 us
    unnamed x1, local copies, waits for them, and re-layouts  1.53 us

profile of v1, /device:TPU:0, one launch (start us, length us, event | category | flops | bytes accessed | tf_op | source)
XLA Modules:
  0.0 40.8 jit_solution(15535349741313527520)
XLA Ops:
  0.0 39.2 %shard_map.73 = bf16[2,32,640]{2,1,0:T(8,128)(2,1)} custom-call(bf16[2,32,640]{2,1,0:T(8,128)(2,1)} %spec_ref.1, bf16[2,1280,640]{2,1,0:T(8,128)(2,1)} %leg_hbm.1, bf16[128,128]{1,0:T(8,128)(2,1)} %constant.4.clone.perm_ref, f32[4]{0:T(128)} %share_ref.1, f32[1280]{0:T(1024)} %quad_ref.1, f32[1280]{0:T(1024)} %constant.5.clone.cor_ref, s32[2]{0:T(128)} %wave_ref.1), custom_call_target="tpu_custom_call" | custom-call | tf_op jit(solution)/shard_map/pallas_call | solution.py:406
  39.2 1.5 %copy.9 = bf16[2,32,640]{2,1,0:T(8,128)(2,1)} copy(bf16[2,32,640]{2,1,0:T(8,128)(2,1)} %shard_map.73) | data formatting | bytes 163840

commit v2 on v1

--- a/solution.py
+++ b/solution.py
@@ -9,7 +9,8 @@
 from jax.experimental.pallas import tpu as pltpu
 from jax.sharding import PartitionSpec as P
 
-TILES = 4
+TILES = 10
+SUB = 2
 LANES = 128
 NT = (((1,), (1,)), ((), ()))
 
@@ -72,6 +73,38 @@
         send_ref[place] = jnp.concatenate([low, high], 0).astype(jnp.bfloat16)
 
 
+def whereabouts(dims, device, number):
+    quarter, block = dims["quarter"], dims["block"]
+    local = [number * block + u for u in range(block)]
+    dist = [
+        jnp.where(
+            r < quarter, device * quarter + r, dims["half"] - (device + 2) * quarter + r
+        )
+        for r in local
+    ]
+    lengths = [20 + 4 * q for q in dist]
+    return local, dist, lengths, [length.astype(jnp.float32) for length in lengths]
+
+
+def trig_stage(dims, device, waves, base, step):
+    rows = dims["slots"] * dims["groups"]
+    all_waves = jnp.concatenate(waves, 0)
+    lane = lax.broadcasted_iota(jnp.int32, (rows, LANES), 1).astype(jnp.float32)
+
+    def group(number, carry):
+        floats = whereabouts(dims, device, number)[3]
+        for u, length in enumerate(floats):
+            inverse = 1.0 / jnp.full((rows, LANES), length, jnp.float32)
+            begin = turn_trig(all_waves * lane, length, inverse)
+            hop = turn_trig(all_waves * float(LANES), length, inverse)
+            for part in range(2):
+                base[number, part, u * rows : (u + 1) * rows, :] = begin[part]
+                step[number, part, u * rows : (u + 1) * rows, :] = hop[part]
+        return carry
+
+    lax.fori_loop(0, 2 * dims["quarter"] // dims["block"], group, 0)
+
+
 def grid_stage(dims, device, waves, quad_ref, cor_ref, get_ref, put_refs, scratch):
     slots, groups, half = dims["slots"], dims["groups"], dims["half"]
     fields, layers, quarter = dims["fields"], dims["layers"], dims["quarter"]
@@ -79,12 +112,11 @@
     count = 2 * quarter
     width = fields * 2 * layers
     depth = 2 * slots * groups
-    state, step, tab, left, mixed, acc = scratch
+    base, step, state, tab, left, mixed, acc = scratch
     chunk = TILES * LANES
     lane = lax.broadcasted_iota(jnp.int32, (groups, LANES), 1)
     south_lane = lane // layers % 2 == 1
     tile_lane = lax.broadcasted_iota(jnp.int32, (slots * groups, LANES), 1)
-    tile_lane_f = tile_lane.astype(jnp.float32)
     hemi_row = lax.broadcasted_iota(jnp.int32, (2 * layers, 1), 0) < layers
     size = block * width
     padded = left.shape[0]
@@ -93,25 +125,10 @@
         == lax.broadcasted_iota(jnp.int32, (padded, padded), 1)
     ).astype(jnp.bfloat16)
     mixed[...] = jnp.zeros_like(mixed)
-    all_waves = jnp.concatenate(waves, 0)
 
     def group(number, carry):
-        first = number * block
-        local = [first + u for u in range(block)]
-        dist = [
-            jnp.where(r < quarter, device * quarter + r, half - device * quarter - count + r)
-            for r in local
-        ]
-        lengths = [20 + 4 * q for q in dist]
-        floats = [length.astype(jnp.float32) for length in lengths]
+        local, dist, lengths, floats = whereabouts(dims, device, number)
         for u in range(block):
-            inverse = 1.0 / jnp.full((slots * groups, LANES), floats[u], jnp.float32)
-            rows = pl.ds(u * slots * groups, slots * groups)
-            base = turn_trig(all_waves * tile_lane_f, floats[u], inverse)
-            hop = turn_trig(all_waves * float(LANES), floats[u], inverse)
-            for part in range(2):
-                state[part, rows, :] = base[part]
-                step[part, rows, :] = hop[part]
             north = get_ref[pl.ds(local[u], groups, stride=count), :]
             south = get_ref[pl.ds(count - 1 - local[u], groups, stride=count), :]
             both = jnp.where(south_lane, south, north)
@@ -137,51 +154,66 @@
             eye, mixed[...].astype(jnp.bfloat16), NT, preferred_element_type=jnp.float32
         ).astype(jnp.bfloat16)
         acc[...] = jnp.zeros_like(acc)
+        state[...] = base[number]
         cor = [
             jnp.where(hemi_row, cor_ref[dist[u]], cor_ref[total_lat - 1 - dist[u]])
             for u in range(block)
         ]
 
         def walk(index, carry):
-            cosine, sine = state[0], state[1]
-            turn_cos, turn_sin = step[0], step[1]
-            for t in range(TILES):
-                start = index * chunk + t * LANES
-                point = tile_lane + start
+            turn_cos, turn_sin = step[number, 0], step[number, 1]
+
+            def fill(t, cosine, sine):
+                point = tile_lane + (index * chunk + t * LANES)
+                cols = slice(t * LANES, (t + 1) * LANES)
                 for u in range(block):
                     rows = slice(u * slots * groups, (u + 1) * slots * groups)
                     live = point < lengths[u]
-                    cols = slice(t * LANES, (t + 1) * LANES)
                     low = u * depth
                     mid = low + slots * groups
                     tab[low:mid, cols] = jnp.where(live, cosine[rows], 0.0).astype(jnp.bfloat16)
                     tab[mid : low + depth, cols] = jnp.where(live, sine[rows], 0.0).astype(
                         jnp.bfloat16
                     )
-                cosine, sine = (
+                return (
                     cosine * turn_cos - sine * turn_sin,
                     sine * turn_cos + cosine * turn_sin,
                 )
+
+            def use(first, last):
+                table = tab[:, first * LANES : last * LANES]
+                grid = jnp.dot(left[...], table, preferred_element_type=jnp.float32)
+                made = []
+                for u in range(block):
+                    part = [
+                        grid[u * width + f * 2 * layers : u * width + (f + 1) * 2 * layers]
+                        for f in range(fields)
+                    ]
+                    absolute = part[2] + cor[u]
+                    made += [
+                        absolute * part[0],
+                        absolute * part[1],
+                        0.5 * (part[0] * part[0] + part[1] * part[1]),
+                        part[0] * part[3],
+                    ]
+                if padded > size:
+                    made.append(jnp.zeros((padded - size, table.shape[1]), jnp.float32))
+                products = jnp.concatenate(made, 0).astype(jnp.bfloat16)
+                return lax.dot_general(table, products, NT, preferred_element_type=jnp.float32)
+
+            cosine, sine = state[0], state[1]
+            total = acc[...]
+            edges = list(range(0, TILES, SUB)) + [TILES]
+            spans = list(zip(edges[:-1], edges[1:]))
+            for t in range(*spans[0]):
+                cosine, sine = fill(t, cosine, sine)
+            for span, following in zip(spans, spans[1:] + [None]):
+                if following:
+                    for t in range(*following):
+                        cosine, sine = fill(t, cosine, sine)
+                total = total + use(*span)
             state[0], state[1] = cosine, sine
-            table = tab[...]
-            grid = jnp.dot(left[...], table, preferred_element_type=jnp.float32)
-            made = []
-            for u in range(block):
-                part = [
-                    grid[u * width + f * 2 * layers : u * width + (f + 1) * 2 * layers]
-                    for f in range(fields)
-                ]
-                absolute = part[2] + cor[u]
-                made += [
-                    absolute * part[0],
-                    absolute * part[1],
-                    0.5 * (part[0] * part[0] + part[1] * part[1]),
-                    part[0] * part[3],
-                ]
-            if padded > size:
-                made.append(jnp.zeros((padded - size, chunk), jnp.float32))
-            products = jnp.concatenate(made, 0).astype(jnp.bfloat16)
-            acc[...] += lax.dot_general(table, products, NT, preferred_element_type=jnp.float32)
+            acc[...] = total
             return carry
 
         longest = lengths[-1]
@@ -216,8 +248,10 @@
     slots, groups, block = dims["slots"], dims["groups"], dims["block"]
     rows = block * slots * groups
     padded = -(-block * dims["fields"] * 2 * dims["layers"] // LANES) * LANES
+    number = 2 * dims["quarter"] // block
     return [
-        pltpu.VMEM((2, rows, LANES), jnp.float32),
+        pltpu.VMEM((number, 2, rows, LANES), jnp.float32),
+        pltpu.VMEM((number, 2, rows, LANES), jnp.float32),
         pltpu.VMEM((2, rows, LANES), jnp.float32),
         pltpu.VMEM((2 * rows, TILES * LANES), jnp.bfloat16),
         pltpu.VMEM((padded, 2 * rows), jnp.bfloat16),
@@ -326,6 +360,8 @@
                 geo[slot, at : at + 1, :] = total
             at = slot * 2 + part
             sum_send[at : at + 1, :] = total
+    fourier_stage(dims, spec_ref, leg, loads, live, perm_ref, rows)
+    split_rows(dims, rows, send)
     pl.semaphore_wait(barrier, groups - 1 + floors - 1)
 
     def wave_place(device):
@@ -333,18 +369,17 @@
 
     tell = exchange("wave", lambda _: wave_send, wave_place, (sem_a, sem_b))
     lift = exchange("lev", lambda _: sum_send, lambda p: sum_recv.at[p], (sem_c, sem_d))
-    for copy in tell + lift:
+    for copy in tell:
         copy.start()
     wave_recv[pl.ds(pl.multiple_of(me * 8, 8), 8), :] = own
-    fourier_stage(dims, spec_ref, leg, loads, live, perm_ref, rows)
-    split_rows(dims, rows, send)
     there = exchange("wave", lambda p: send.at[p], lambda p: recv.at[p], (sem_e, sem_f))
-    for copy in there:
+    for copy in there + lift:
         copy.start()
     recv[me] = send[me]
     for copy in tell:
         copy.wait()
     waves = [wave_recv[pl.ds(slot, groups, stride=8), :] for slot in range(slots)]
+    trig_stage(dims, me, waves, scratch[0], scratch[1])
     for copy in there:
         copy.wait()
     for source in range(groups):

time: 40.9 us -> 34.5 us (0.84)
  Pallas kernels: 39.2 us -> 32.8 us
    pallas_call x1, Pallas kernels: 39.2 us -> 32.8 us  [body(): pl.pallas_call(functools.partial(whole_kernel, dims), out_shape=jax.Shape...]
where the time goes in v2:
time: 34.5 us; the launch traced here: 34.3 us
  Pallas kernels  32.8 us (95%)
  local copies, waits for them, and re-layouts  1.53 us (4%)
    pallas_call x1, Pallas kernels, body(): pl.pallas_call(functools.partial(whole_kernel, dims), out_shape=jax.Shape...  32.8 us
    unnamed x1, local copies, waits for them, and re-layouts  1.53 us

profile of v2, /device:TPU:0, one launch (start us, length us, event | category | flops | bytes accessed | tf_op | source)
XLA Modules:
  0.0 34.3 jit_solution(9073296319635024537)
XLA Ops:
  0.0 32.8 %shard_map.73 = bf16[2,32,640]{2,1,0:T(8,128)(2,1)} custom-call(bf16[2,32,640]{2,1,0:T(8,128)(2,1)} %spec_ref.1, bf16[2,1280,640]{2,1,0:T(8,128)(2,1)} %leg_hbm.1, bf16[128,128]{1,0:T(8,128)(2,1)} %constant.4.clone.perm_ref, f32[4]{0:T(128)} %share_ref.1, f32[1280]{0:T(1024)} %quad_ref.1, f32[1280]{0:T(1024)} %constant.5.clone.cor_ref, s32[2]{0:T(128)} %wave_ref.1), custom_call_target="tpu_custom_call" | custom-call | tf_op jit(solution)/shard_map/pallas_call | solution.py:441
  32.8 1.5 %copy.9 = bf16[2,32,640]{2,1,0:T(8,128)(2,1)} copy(bf16[2,32,640]{2,1,0:T(8,128)(2,1)} %shard_map.73) | data formatting | bytes 163840
